TPU v7x, 32 devices: a whole 2x2x4 slice. The times are simulated.
32 devices in a mesh: lat: 4 (over z), lon: 4 (over y, x), rad: 2 (over core).
Axes of the slice: x: 2, y: 2, z: 4, core: 2. Of those that a mesh axis runs over, the one named last changes fastest.
Arguments:
- velocity: float32 [3, 32, 32, 1024], P(None, 'rad', 'lat', 'lon'), may hold values from -6 to 6
- forcing: float32 [3, 32, 32, 1024], P(None, 'rad', 'lat', 'lon'), may hold values from -6 to 6
- viscosity: float32 [32, 32, 1024], P('rad', 'lat', 'lon'), may hold values from 0.1 to 10
- plate_ids: int32 [4, 128], P('lat', 'lon'), may hold values from 0 to 11, as said below
Outputs:
- new_velocity: float32 [3, 32, 32, 1024], P(None, 'rad', 'lat', 'lon')
- coarse_residual: float32 [3, 16, 16, 512], P(None, None, 'lat', 'lon')
- plate_velocity: float32 [3, 32, 1024], P(None, 'lat', 'lon')
Inputs may be any that keep to these rules, and one draw needn't show every extreme that they name: `plate_ids`: every plate number from 0 to 11 names at least one face block.
All inputs are finite; a program needn't handle non-finite values.
Results may differ from a plain program's by a relative error of at most 0.0003.
Values sent between devices are 32-bit elements; how exact they have to be, the bound alone decides.
A program may use at most 64 MiB of HBM per device.

v0:
```python
import jax
import jax.numpy as jnp
from jax import lax
from jax.sharding import PartitionSpec as P

SWEEPS = 3
PLATES = 12
FACE = 8


relaxation = 0.8
neighbours = ((0, 1, 1), (2, 1, 1), (1, 0, 1), (1, 2, 1), (1, 1, 0), (1, 1, 2))


def padded(block, sides, width, periodic):
    for axis, dim in sides:
        count = lax.axis_size(axis)
        forward = [(i, i + 1) for i in range(count - 1)]
        if periodic:
            forward.append((count - 1, 0))
        backward = [(target, source) for source, target in forward]
        low = lax.ppermute(
            lax.slice_in_dim(block, block.shape[dim] - width, None, axis=dim), axis, forward
        )
        high = lax.ppermute(lax.slice_in_dim(block, 0, width, axis=dim), axis, backward)
        block = jnp.concatenate([low, block, high], axis=dim)
    return block


def harmonic(own_visc, other_visc):
    total = own_visc + other_visc
    positive = total > 0
    safe_total = jnp.where(positive, total, 1.0)
    return jnp.where(positive, 2.0 * own_visc * other_visc / safe_total, 0.0)


def operate(padded_vel, padded_visc):
    center_vel = padded_vel[:, 1:-1, 1:-1, 1:-1]
    own_visc = padded_visc[1:-1, 1:-1, 1:-1]
    count_rad, count_lat, count_lon = own_visc.shape
    action = 0.5 * own_visc * center_vel
    diagonal = 0.5 * own_visc
    for step_rad, step_lat, step_lon in neighbours:
        other_visc = padded_visc[
            step_rad : step_rad + count_rad,
            step_lat : step_lat + count_lat,
            step_lon : step_lon + count_lon,
        ]
        other_vel = padded_vel[
            :,
            step_rad : step_rad + count_rad,
            step_lat : step_lat + count_lat,
            step_lon : step_lon + count_lon,
        ]
        link_weight = harmonic(own_visc, other_visc)
        diagonal = diagonal + link_weight
        action = action + link_weight * (center_vel - other_vel)
    return (action, diagonal, center_vel, own_visc)


def relax_step(padded_vel, forcing_in, padded_visc):
    action, diagonal, center_vel, own_visc = operate(padded_vel, padded_visc)
    inside = own_visc > 0
    safe_diag = jnp.where(inside, diagonal, 1.0)
    updated = center_vel + relaxation * (forcing_in - action) / safe_diag
    return jnp.where(inside, updated, center_vel)


def restrict(residual_field):
    shape_all = residual_field.shape
    blocks = residual_field.reshape(
        shape_all[0], shape_all[1] // 2, 2, shape_all[2] // 2, 2, shape_all[3] // 2, 2
    )
    return jnp.mean(blocks, axis=(2, 4, 6))


def surface(velocity, viscosity, lat_cells, lon_cells, lat_total, lon_total):
    latitude = jnp.pi * ((lat_cells + 0.5) / lat_total - 0.5)
    longitude = 2.0 * jnp.pi * (lon_cells + 0.5) / lon_total
    lon_ones = jnp.ones_like(longitude)[None, :]
    cos_lat = jnp.cos(latitude)[:, None] * lon_ones
    radius_x = cos_lat * jnp.cos(longitude)[None, :]
    radius_y = cos_lat * jnp.sin(longitude)[None, :]
    radius_z = jnp.sin(latitude)[:, None] * lon_ones
    traction = viscosity[-1][None] * (velocity[:, -1] - velocity[:, -2])
    torque = jnp.stack(
        [
            (radius_y * traction[2] - radius_z * traction[1]) * cos_lat,
            (radius_z * traction[0] - radius_x * traction[2]) * cos_lat,
            (radius_x * traction[1] - radius_y * traction[0]) * cos_lat,
            cos_lat,
        ]
    )
    return (torque, (radius_x, radius_y, radius_z))


def plate_table(plate_ids):
    cell_plates = jnp.repeat(jnp.repeat(plate_ids, FACE, axis=0), FACE, axis=1)
    numbers = jnp.arange(PLATES, dtype=jnp.int32)[:, None, None]
    onehot = (cell_plates[None] == numbers).astype(jnp.float32)
    return onehot.reshape(PLATES, -1)


def rotate(rotation, onehot, radius):
    per_cell = jnp.dot(rotation, onehot, precision=lax.Precision.HIGHEST).reshape(
        (3,) + radius[0].shape
    )
    radius_x, radius_y, radius_z = radius
    return jnp.stack(
        [
            per_cell[1] * radius_z - per_cell[2] * radius_y,
            per_cell[2] * radius_x - per_cell[0] * radius_z,
            per_cell[0] * radius_y - per_cell[1] * radius_x,
        ]
    )


def shrink_by(block, margin):
    shape_all = block.shape
    return block[
        ...,
        margin : shape_all[-3] - margin,
        margin : shape_all[-2] - margin,
        margin : shape_all[-1] - margin,
    ]


def extend_deep(stacked, width):
    sided = padded(stacked, (("lon", 3),), width, True)
    return padded(sided, (("lat", 2), ("rad", 1)), width, False)


def on_device(velocity, forcing, viscosity, plate_ids):
    width = SWEEPS + 1
    packed = extend_deep(jnp.concatenate([velocity, forcing, viscosity[None]], 0), width)
    wide_vel = packed[:3]
    wide_force = packed[3:6]
    wide_visc = packed[6]
    for sweep_index in range(SWEEPS):
        wide_vel = relax_step(
            wide_vel, shrink_by(wide_force, sweep_index + 1), shrink_by(wide_visc, sweep_index)
        )
    action = operate(wide_vel, shrink_by(wide_visc, SWEEPS))[0]
    residual_field = shrink_by(wide_force, width) - action
    current = wide_vel[:, 1:-1, 1:-1, 1:-1]
    coarse_residual = lax.all_gather(restrict(residual_field), "rad", axis=1, tiled=True)
    count_lat = velocity.shape[2]
    count_lon = velocity.shape[3]
    lat_cells = (lax.axis_index("lat") * count_lat + jnp.arange(count_lat, dtype=jnp.int32)).astype(
        jnp.float32
    )
    lon_cells = (lax.axis_index("lon") * count_lon + jnp.arange(count_lon, dtype=jnp.int32)).astype(
        jnp.float32
    )
    torque, radius = surface(
        current,
        viscosity,
        lat_cells,
        lon_cells,
        count_lat * lax.axis_size("lat"),
        count_lon * lax.axis_size("lon"),
    )
    onehot = plate_table(plate_ids)
    is_top = (lax.axis_index("rad") == lax.axis_size("rad") - 1).astype(jnp.float32)
    partial_sums = (
        jnp.dot(torque.reshape(4, -1), onehot.T, precision=lax.Precision.HIGHEST) * is_top
    )
    sums = lax.psum(partial_sums, ("lat", "lon", "rad"))
    rotation = sums[:3] / jnp.sqrt(sums[3])[None]
    return (current, coarse_residual, rotate(rotation, onehot, radius))


def solution(mesh):
    placed = (
        P(None, "rad", "lat", "lon"),
        P(None, "rad", "lat", "lon"),
        P("rad", "lat", "lon"),
        P("lat", "lon"),
    )
    return jax.shard_map(
        on_device,
        mesh=mesh,
        in_specs=placed,
        out_specs=(
            P(None, "rad", "lat", "lon"),
            P(None, None, "lat", "lon"),
            P(None, "lat", "lon"),
        ),
        check_vma=False,
    )
```

profile of v0, /device:TPU:0, one launch (start us, length us, event | category | flops | bytes accessed | tf_op | source)
XLA Modules:
  0.0 161.3 jit_solution(13120766126010251404)
XLA Ops:
  0.7 1.3 pad_maximum_fusion.2
  2.2 3.0 %collective-permute-start = (f32[7,16,8,4]{3,2,0,1:T(8,128)S(1)}, f32[7,16,8,4]{3,2,0,1:T(8,128)S(1)}, u32[]{:S(2)}, u32[]{:S(2)}) collective-permute-start(f32[7,16,8,4]{3,2,0,1:T(8,128)S(1)} %get-tuple-element.48), channel_id=1, source_target_pairs={{0,2},{2,4},{4,6},{6,0},{1,3},{3,5},{5,7},{7,1},{8,10},{10,12},{12... | collective-permute-start | bytes 43016 | tf_op jit(solution)/shard_map/ppermute | solution.py:22
  5.2 1.0 collective-permute-start.1
  6.2 11.3 %collective-permute-done = f32[7,16,8,4]{3,2,0,1:T(8,128)S(1)} collective-permute-done((f32[7,16,8,4]{3,2,0,1:T(8,128)S(1)}, f32[7,16,8,4]{3,2,0,1:T(8,128)S(1)}, u32[]{:S(2)}, u32[]{:S(2)}) %collective-permute-start) | collective-permute-done | bytes 14368 | tf_op jit(solution)/shard_map/ppermute | solution.py:22
  17.5 9.2 %collective-permute-done.1 = f32[7,16,8,4]{3,2,0,1:T(8,128)S(1)} collective-permute-done((f32[7,16,8,4]{3,2,0,1:T(8,128)S(1)}, f32[7,16,8,4]{3,2,0,1:T(8,128)S(1)}, u32[]{:S(2)}, u32[]{:S(2)}) %collective-permute-start.1) | collective-permute-done | bytes 14368 | tf_op jit(solution)/shard_map/ppermute | solution.py:25
  27.5 0.9 copy.35
  28.4 1.3 collective-permute-start.3
  29.7 0.9 copy.34
  30.7 5.4 %collective-permute-start.2 = (f32[7,16,4,264]{3,1,2,0:T(8,128)}, f32[7,16,4,264]{3,1,2,0:T(8,128)}, u32[]{:S(2)}, u32[]{:S(2)}) collective-permute-start(f32[7,16,4,264]{3,1,2,0:T(8,128)} %copy.34), channel_id=1, source_target_pairs={{0,8},{8,16},{16,24},{1,9},{9,17},{17,25},{2,10},{10,18},{18,26},{... | collective-permute-start | bytes 1419272 | tf_op jit(solution)/shard_map/ppermute | solution.py:22
  36.2 10.6 %collective-permute-done.3 = f32[7,16,4,264]{3,1,2,0:T(8,128)S(1)} collective-permute-done((f32[7,16,4,264]{3,1,2,0:T(8,128)}, f32[7,16,4,264]{3,1,2,0:T(8,128)S(1)}, u32[]{:S(2)}, u32[]{:S(2)}) %collective-permute-start.3) | collective-permute-done | bytes 473120 | tf_op jit(solution)/shard_map/ppermute | solution.py:25
  47.1 1.9 %collective-permute-done.2 = f32[7,16,4,264]{3,1,2,0:T(8,128)} collective-permute-done((f32[7,16,4,264]{3,1,2,0:T(8,128)}, f32[7,16,4,264]{3,1,2,0:T(8,128)}, u32[]{:S(2)}, u32[]{:S(2)}) %collective-permute-start.2) | collective-permute-done | bytes 473120 | tf_op jit(solution)/shard_map/ppermute | solution.py:22
  49.1 1.4 copy.36
  51.0 0.9 copy.38
  51.9 0.9 copy.39
  52.9 1.3 collective-permute-start.5
  54.2 4.8 %collective-permute-start.4 = (f32[7,4,16,264]{3,2,1,0:T(8,128)}, f32[7,4,16,264]{3,2,1,0:T(8,128)}, u32[]{:S(2)}, u32[]{:S(2)}) collective-permute-start(f32[7,4,16,264]{3,2,1,0:T(8,128)} %copy.38), channel_id=1, source_target_pairs={{0,1},{2,3},{4,5},{6,7},{8,9},{10,11},{12,13},{14,15},{16,17},{18,... | collective-permute-start | bytes 1419272 | tf_op jit(solution)/shard_map/ppermute | solution.py:22
  59.0 1.1 collective-permute-done.4
  60.1 5.2 %pad_maximum_fusion = f32[7,24,16,264]{3,2,0,1:T(8,128)S(1)} fusion(f32[7,16,4,264]{3,2,0,1:T(4,128)S(1)} %copy.37, f32[7,16,8,4]{3,2,0,1:T(8,128)S(1)} %collective-permute-done.1, f32[1,16,8,256]{3,2,0,1:T(8,128)S(1)} %bitcast.24, f32[7,16,8,4]{3,2,0,1:T(8,128)S(1)} %collective-permute-done, f32[7,16,4,264]{3,2,0,1:T(4,128)S(1)} %copy.36, ...), kind=kLoop, calls=%fused_computation | loop fusion | flops 5677056 | bytes 5677056 | tf_op jit(solution)/shard_map/concatenate | solution.py:26
  65.7 1.1 add_select_fusion.5
  66.8 1.2 add_select_fusion.4
  68.0 1.3 add_select_fusion.3
  69.2 3.7 %add_select_fusion = f32[3,22,14,262]{3,2,0,1:T(8,128)S(1)} fusion(f32[7,24,16,264]{3,2,0,1:T(8,128)S(1)} %pad_maximum_fusion, f32[22,14,262]{2,1,0:T(8,128)S(1)} %get-tuple-element.34, f32[22,14,262]{2,1,0:T(8,128)S(1)} %get-tuple-element.40, f32[22,14,262]{2,1,0:T(8,128)S(1)} %get-tuple-element.39, f32[22,14,262]{2,1,0:T(8,128)S(1)} %get-tuple-element.38, ...), kind=kLoop, calls=%fused_computation.1 | loop fusion | flops 5810112 | bytes 11378136 | tf_op jit(solution)/shard_map/jit(_where)/select_n | solution.py:66
  72.9 3.4 %add_select_fusion.1 = f32[3,20,12,260]{3,2,0,1:T(8,128)S(1)} fusion(f32[3,22,14,262]{3,2,0,1:T(8,128)S(1)} %add_select_fusion, f32[7,24,16,264]{3,2,0,1:T(8,128)S(1)} %pad_maximum_fusion, f32[20,12,260]{2,1,0:T(8,128)S(1)} %get-tuple-element.26, f32[20,12,260]{2,1,0:T(8,128)S(1)} %get-tuple-element.32, f32[20,12,260]{2,1,0:T(8,128)S(1)} %get-tuple-element.31, ...), kind=kLoop, calls=%fused_computation.2 | loop fusion | flops 4492800 | bytes 8798400 | tf_op jit(solution)/shard_map/jit(_where)/select_n | solution.py:66
  76.3 3.0 %add_select_fusion.2 = f32[3,18,10,258]{3,2,0,1:T(8,128)S(1)} fusion(f32[3,20,12,260]{3,2,0,1:T(8,128)S(1)} %add_select_fusion.1, f32[7,24,16,264]{3,2,0,1:T(8,128)S(1)} %pad_maximum_fusion, f32[18,10,258]{2,1,0:T(8,128)S(1)} %get-tuple-element.18, f32[18,10,258]{2,1,0:T(8,128)S(1)} %get-tuple-element.24, f32[18,10,258]{2,1,0:T(8,128)S(1)} %get-tuple-element.23, ...), kind=kLoop, calls=%fused_computation.3 | loop fusion | flops 3343680 | bytes 6548040 | tf_op jit(solution)/shard_map/jit(_where)/select_n | solution.py:66
  79.4 0.7 fusion.66
  80.5 40.6 %psum.7 = f32[4,12]{1,0:T(4,128)S(1)} all-reduce(f32[4,12]{1,0:T(4,128)S(1)} %fusion.45), channel_id=1, replica_groups=mesh['lat'=4,'lon'=4,'rad'=2] {'lat','lon','rad'}, use_global_device_ids=true, to_apply=%region_1.2 | all-reduce | flops 48 | bytes 384 | tf_op jit(solution)/shard_map/psum | solution.py:168
  121.4 0.8 copy.45
  122.2 26.5 %reshape.492 = f32[3,8,2,4,2,128,2]{6,5,4,3,2,1,0:T(8,128)} reshape(f32[3,16,8,256]{3,2,1,0:T(8,128)S(1)} %copy.43) | data formatting | bytes 786432 | tf_op jit(solution)/shard_map/reshape | solution.py:71
  148.6 9.4 %reduce_sum.9 = f32[3,8,4,128]{3,2,1,0:T(4,128)S(1)} reduce(f32[3,8,2,4,2,128,2]{6,5,4,3,2,1,0:T(8,128)} %reshape.492, f32[]{:T(128)} %constant.15.clone.1), dimensions={2,4,6}, to_apply=%region_0.1 | reduce | flops 86016 | bytes 442372 | tf_op jit(solution)/shard_map/reduce_sum | solution.py:74
  158.1 1.9 %all_gather.3 = f32[3,16,4,128]{3,2,1,0:T(4,128)S(1)} all-gather(f32[3,8,4,128]{3,2,1,0:T(4,128)S(1)} %broadcast_multiply_fusion), channel_id=1, replica_groups=mesh['lat'=4,'lon'=4,'rad'=2] {'rad'}, dimensions={1}, use_global_device_ids=true | all-gather | bytes 147456 | tf_op jit(solution)/shard_map/all_gather | solution.py:146
  160.0 0.6 pad_maximum_fusion.11
  160.7 0.6 copy.71
  (37 shorter events, 3.2 us)
Async XLA Ops:
  0.6 26.1 %copy-start = (f32[3,16,8,256]{3,2,1,0:T(8,128)S(1)}, f32[3,16,8,256]{3,2,1,0:T(8,128)}, u32[]{:S(2)}) copy-start(f32[3,16,8,256]{3,2,1,0:T(8,128)} %param.5) | copy-start | bytes 1179652
  0.6 26.1 %copy-start.1 = (f32[3,16,8,256]{3,2,1,0:T(8,128)S(1)}, f32[3,16,8,256]{3,2,1,0:T(8,128)}, u32[]{:S(2)}) copy-start(f32[3,16,8,256]{3,2,1,0:T(8,128)} %param.4) | copy-start | bytes 1179652
  0.7 26.1 %copy-start.2 = (f32[16,8,256]{2,1,0:T(8,128)S(1)}, f32[16,8,256]{2,1,0:T(8,128)}, u32[]{:S(2)}) copy-start(f32[16,8,256]{2,1,0:T(8,128)} %param.6) | copy-start | bytes 393220
  2.2 15.3 %collective-permute-start = (f32[7,16,8,4]{3,2,0,1:T(8,128)S(1)}, f32[7,16,8,4]{3,2,0,1:T(8,128)S(1)}, u32[]{:S(2)}, u32[]{:S(2)}) collective-permute-start(f32[7,16,8,4]{3,2,0,1:T(8,128)S(1)} %get-tuple-element.48), channel_id=1, source_target_pairs={{0,2},{2,4},{4,6},{6,0},{1,3},{3,5},{5,7},{7,1},{8,10},{10,12},{12... | collective-permute-start | bytes 43016 | tf_op jit(solution)/shard_map/ppermute | solution.py:22
  5.2 21.6 %collective-permute-start.1 = (f32[7,16,8,4]{3,2,0,1:T(8,128)S(1)}, f32[7,16,8,4]{3,2,0,1:T(8,128)S(1)}, u32[]{:S(2)}, u32[]{:S(2)}) collective-permute-start(f32[7,16,8,4]{3,2,0,1:T(8,128)S(1)} %get-tuple-element.49), channel_id=1, source_target_pairs={{2,0},{4,2},{6,4},{0,6},{3,1},{5,3},{7,5},{1,7},{10,8},{12,10},{14... | collective-permute-start | bytes 43016 | tf_op jit(solution)/shard_map/ppermute | solution.py:25
  27.5 8.6 %copy-start.3 = (s32[1,32]{1,0:T(1,128)S(1)}, s32[1,32]{1,0:T(1,128)}, u32[]{:S(2)}) copy-start(s32[1,32]{1,0:T(1,128)} %param.7) | copy-start | bytes 388
  28.4 18.4 %collective-permute-start.3 = (f32[7,16,4,264]{3,1,2,0:T(8,128)}, f32[7,16,4,264]{3,1,2,0:T(8,128)S(1)}, u32[]{:S(2)}, u32[]{:S(2)}) collective-permute-start(f32[7,16,4,264]{3,1,2,0:T(8,128)} %copy.35), channel_id=1, source_target_pairs={{8,0},{16,8},{24,16},{9,1},{17,9},{25,17},{10,2},{18,10},{26,18},{... | collective-permute-start | bytes 1419272 | tf_op jit(solution)/shard_map/ppermute | solution.py:25
  30.7 18.4 %collective-permute-start.2 = (f32[7,16,4,264]{3,1,2,0:T(8,128)}, f32[7,16,4,264]{3,1,2,0:T(8,128)}, u32[]{:S(2)}, u32[]{:S(2)}) collective-permute-start(f32[7,16,4,264]{3,1,2,0:T(8,128)} %copy.34), channel_id=1, source_target_pairs={{0,8},{8,16},{16,24},{1,9},{9,17},{17,25},{2,10},{10,18},{18,26},{... | collective-permute-start | bytes 1419272 | tf_op jit(solution)/shard_map/ppermute | solution.py:22
  52.9 6.2 %collective-permute-start.5 = (f32[7,4,16,264]{3,2,1,0:T(8,128)}, f32[7,4,16,264]{3,2,1,0:T(8,128)}, u32[]{:S(2)}, u32[]{:S(2)}) collective-permute-start(f32[7,4,16,264]{3,2,1,0:T(8,128)} %copy.39), channel_id=1, source_target_pairs={{1,0},{3,2},{5,4},{7,6},{9,8},{11,10},{13,12},{15,14},{17,16},{19,... | collective-permute-start | bytes 1419272 | tf_op jit(solution)/shard_map/ppermute | solution.py:25
  54.2 6.0 %collective-permute-start.4 = (f32[7,4,16,264]{3,2,1,0:T(8,128)}, f32[7,4,16,264]{3,2,1,0:T(8,128)}, u32[]{:S(2)}, u32[]{:S(2)}) collective-permute-start(f32[7,4,16,264]{3,2,1,0:T(8,128)} %copy.38), channel_id=1, source_target_pairs={{0,1},{2,3},{4,5},{6,7},{8,9},{10,11},{12,13},{14,15},{16,17},{18,... | collective-permute-start | bytes 1419272 | tf_op jit(solution)/shard_map/ppermute | solution.py:22
where the time goes:
time: 162 us; the launch traced here: 161 us
  blocking collectives  42.5 us (26%)
  waiting for transfers between devices  34.2 us (21%)
  local copies, waits for them, and re-layouts  34 us (21%)
  other arithmetic  32.6 us (20%)
  starting transfers between devices  16.8 us (10%)
    psum x1, blocking collectives, on_device(): sums = lax.psum(partial_sums, ('lat', 'lon', 'rad'))  40.6 us
    reshape x1, local copies, waits for them, and re-layouts, restrict(): residual_field.reshape(shape_all[0], shape_all[1] // 2, 2, shape_all[2] /...  26.5 us
    ppermute x3, waiting for transfers between devices, padded(): lax.ppermute(lax.slice_in_dim(block, 0, width, axis=dim), axis, backward)  19.9 us
    ppermute x3, waiting for transfers between devices, padded(): lax.ppermute(lax.slice_in_dim(block, block.shape[dim] - width, None, axis...  14.3 us
    ppermute x3, starting transfers between devices, padded(): lax.ppermute(lax.slice_in_dim(block, block.shape[dim] - width, None, axis...  13.2 us
    select_n x3, other arithmetic, relax_step(): return jnp.where(inside, updated, center_vel)  10.1 us
    reduce_sum x1, other arithmetic, restrict(): return jnp.mean(blocks, axis=(2, 4, 6))  9.42 us
    concatenate x2, other arithmetic, padded(): block = jnp.concatenate([low, block, high], axis=dim)  5.72 us
  transfers between devices with their start and end apart: 6, of which 5 were waited for; matrix products, arithmetic and copies ran while one was open for 1% of the time, Pallas kernels for 0%

commit v1 on v0

v1 whole, which is shorter than its diff:
```python
import functools
import math

import jax
import jax.numpy as jnp
from jax import lax
from jax.experimental import pallas as pl
from jax.experimental.pallas import tpu as pltpu
from jax.sharding import PartitionSpec as P

SWEEPS = 3
PLATES = 12
FACE = 8
RELAX = 0.8
COMPS = 3
LANES = 128
SLOT = 32
MESH = pl.DeviceIdType.MESH
HIGHEST = lax.Precision.HIGHEST
UNROLL = 4


def harmonic(own, other):
    return 2.0 * own * other / (own + other)


def kernel(
    sizes, vel, forc, visc, ids,
    newv, coarse, plate,
    v, f, eta, w_lat, w_lon, w_rad, gain, diag,
    face_out, face_in, col_out, col_in, pairs,
    lat_sums, lon_sums, stage_out,
    load_sem, send_sem, recv_sem, s1_send, s1_recv, s2_send, s2_recv, g_send, g_recv, out_sem,
):
    n_lat, n_lon, n_rad = sizes
    n_r, n_a, n_o = visc.shape
    me_lat, me_lon, me_rad = (lax.axis_index(a) for a in ("lat", "lon", "rad"))
    lat_lo, lat_hi = me_lat > 0, me_lat < n_lat - 1
    rad_lo, rad_hi = me_rad > 0, me_rad < n_rad - 1
    lon_up, lon_dn = lax.rem(me_lon + 1, n_lon), lax.rem(me_lon + n_lon - 1, n_lon)
    is_top = me_rad == n_rad - 1

    loads = [
        pltpu.make_async_copy(visc, eta.at[pl.ds(1, n_r)], load_sem.at[0]),
        pltpu.make_async_copy(vel, v.at[0, :, pl.ds(1, n_r)], load_sem.at[1]),
        pltpu.make_async_copy(forc, f, load_sem.at[2]),
    ]
    for load in loads:
        load.start()

    barrier = pltpu.get_barrier_semaphore()

    def greet(device):
        pl.semaphore_signal(barrier, inc=1, device_id=device, device_id_type=MESH)

    expected = 2
    greet({"lon": lon_up})
    greet({"lon": lon_dn})
    for has, device in (
        (lat_lo, {"lat": me_lat - 1}), (lat_hi, {"lat": me_lat + 1}),
        (rad_lo, {"rad": me_rad - 1}), (rad_hi, {"rad": me_rad + 1}),
    ):
        pl.when(has)(functools.partial(greet, device))
        expected = expected + jnp.where(has, 1, 0)
    if n_lat - 1 > SWEEPS + 1:
        for step in range(1, n_lat):
            greet({"lat": lax.rem(me_lat + step, n_lat)})
        expected = expected + (n_lat - 1)
    if n_lon // 2 + n_rad - 1 > SWEEPS + 1:
        for step in range(1, n_lon * n_rad):
            greet({
                "lon": lax.rem(me_lon + step // n_rad, n_lon),
                "rad": lax.rem(me_rad + step % n_rad, n_rad),
            })
        expected = expected + (n_lon * n_rad - 1)

    lane_wide = lax.broadcasted_iota(jnp.int32, (n_a, n_o), 1)
    lane = lax.broadcasted_iota(jnp.int32, (n_a, LANES), 1)
    row = lax.broadcasted_iota(jnp.int32, (n_a, n_o), 0)
    reps = n_o // LANES

    zero_plane = jnp.zeros((n_a, n_o), jnp.float32)
    for has, slot in ((rad_lo, 0), (rad_hi, n_r + 1)):
        @pl.when(jnp.logical_not(has))
        def _():
            eta[slot] = zero_plane
            for t in range(SWEEPS + 1):
                for c in range(COMPS):
                    v[t, c, slot] = zero_plane
    for has, side in ((lat_lo, 0), (lat_hi, 1)):
        @pl.when(jnp.logical_not(has))
        def _():
            for t in range(SWEEPS + 1):
                face_in[t, side] = jnp.zeros(face_in.shape[2:], jnp.float32)

    def links(t):
        rows = pl.ds(0, ((COMPS + 1) if t == 0 else COMPS) * n_r)

        def remote(src, dst, k, device):
            return pltpu.make_async_remote_copy(
                src, dst, send_sem.at[t, k], recv_sem.at[t, k], device_id=device, device_id_type=MESH
            )

        out = [
            (remote(face_out.at[t, 1, rows], face_in.at[t, 0, rows], 0, {"lat": me_lat + 1}), lat_hi, lat_lo),
            (remote(face_out.at[t, 0, rows], face_in.at[t, 1, rows], 1, {"lat": me_lat - 1}), lat_lo, lat_hi),
            (remote(col_out.at[t, 1], col_in.at[t, 0], 2, {"lon": lon_up}), None, None),
            (remote(col_out.at[t, 0], col_in.at[t, 1], 3, {"lon": lon_dn}), None, None),
            (remote(v.at[t, :, n_r], v.at[t, :, 0], 4, {"rad": me_rad + 1}), rad_hi, rad_lo),
            (remote(v.at[t, :, 1], v.at[t, :, n_r + 1], 5, {"rad": me_rad - 1}), rad_lo, rad_hi),
        ]
        if t == 0:
            out += [
                (remote(eta.at[n_r], eta.at[0], 6, {"rad": me_rad + 1}), rad_hi, rad_lo),
                (remote(eta.at[1], eta.at[n_r + 1], 7, {"rad": me_rad - 1}), rad_lo, rad_hi),
            ]
        return out

    def guarded(cond, call):
        if cond is None:
            call()
        else:
            pl.when(cond)(call)

    def start(t):
        for copy, sends, _ in links(t):
            guarded(sends, copy.start)

    def arrive(t):
        for copy, _, receives in links(t):
            guarded(receives, copy.wait_recv)

    def sent(t):
        for copy, sends, _ in links(t):
            guarded(sends, copy.wait_send)

    def pack(t, k, tile, cols):
        face_out[t, 0, k] = tile[:1]
        face_out[t, 1, k] = tile[n_a - 1 :]
        low, high = cols
        hit = lane == k
        low = jnp.where(hit, pltpu.roll(tile[:, :LANES], k, 1), low)
        high = jnp.where(hit, pltpu.roll(tile[:, n_o - LANES :], lax.rem(k + 1, LANES), 1), high)
        return low, high

    def over_radius(body, init):
        def block(i, carry):
            for j in range(UNROLL):
                carry = body(i * UNROLL + j, carry)
            return carry

        return lax.fori_loop(0, n_r // UNROLL, block, init)

    no_cols = (jnp.zeros((n_a, LANES), jnp.float32),) * 2

    def shifted(t, k, tile, cols):
        col_lo, col_hi = cols
        below = jnp.where(row == 0, face_in[t, 0, k], pltpu.roll(tile, 1, 0))
        above = jnp.where(row == n_a - 1, face_in[t, 1, k], pltpu.roll(tile, n_a - 1, 0))
        from_lo = pltpu.roll(col_lo, lax.rem(LANES - k, LANES), 1)
        from_hi = pltpu.roll(col_hi, LANES - 1 - k, 1)
        west = jnp.where(lane_wide == 0, jnp.concatenate([from_lo] * reps, 1), pltpu.roll(tile, 1, 1))
        east = jnp.where(
            lane_wide == n_o - 1, jnp.concatenate([from_hi] * reps, 1), pltpu.roll(tile, n_o - 1, 1)
        )
        return below, above, west, east

    loads[0].wait()
    loads[1].wait()

    def pack_first(r, cols):
        for c in range(COMPS):
            cols = pack(0, c * n_r + r, v[0, c, r + 1], cols)
        return pack(0, COMPS * n_r + r, eta[r + 1], cols)

    low, high = over_radius(pack_first, no_cols)
    col_out[0, 0] = low
    col_out[0, 1] = high
    pl.semaphore_wait(barrier, expected)
    start(0)

    lat_cell = (me_lat * n_a + row).astype(jnp.float32)
    lon_cell = (me_lon * n_o + lane_wide).astype(jnp.float32)
    phi = math.pi * ((lat_cell + 0.5) / (n_lat * n_a) - 0.5)
    lam = (2.0 * math.pi) * (lon_cell[:1] + 0.5) / (n_lon * n_o)
    cos_lat = jnp.cos(phi)
    rx = cos_lat * jnp.cos(lam)
    ry = cos_lat * jnp.sin(lam)
    rz = jnp.sin(phi)
    blocks = ids.shape[1]
    spread_rows = lax.broadcasted_iota(jnp.int32, (blocks, n_o), 0)
    spread_cols = lax.broadcasted_iota(jnp.int32, (blocks, n_o), 1)
    spread = (spread_cols // FACE == spread_rows).astype(jnp.float32)
    numbers = lax.broadcasted_iota(jnp.int32, (SLOT, n_o), 0)
    onehots = []
    for band in range(n_a // FACE):
        own = jnp.broadcast_to(ids[band : band + 1].astype(jnp.float32), (8, blocks))
        cells = jnp.dot(own, spread, precision=HIGHEST)[:1]
        onehots.append((jnp.abs(cells - numbers.astype(jnp.float32)) < 0.5).astype(jnp.float32))

    arrive(0)

    cols_first = (col_in[0, 0], col_in[0, 1])
    w_rad[0] = harmonic(eta[1], eta[0])

    def weigh(r, carry):
        own = eta[r + 1]
        near = shifted(0, COMPS * n_r + r, own, cols_first)
        below, above, west, east = (harmonic(own, other) for other in near)
        up = harmonic(own, eta[r + 2])
        w_lat[0, r] = below
        w_lat[1, r] = above
        w_lon[0, r] = west
        w_lon[1, r] = east
        w_rad[r + 1] = up
        d = 0.5 * own + (below + above) + (west + east) + (up + w_rad[r])
        diag[r] = d
        gain[r] = RELAX / d
        return carry

    over_radius(weigh, 0)
    loads[2].wait()

    def flux(t, c, r, cols):
        tile = v[t, c, r + 1]
        below, above, west, east = shifted(t, c * n_r + r, tile, cols)
        total = (
            (w_lat[0, r] * below + w_lat[1, r] * above)
            + (w_lon[0, r] * west + w_lon[1, r] * east)
            + (w_rad[r] * v[t, c, r] + w_rad[r + 1] * v[t, c, r + 2])
        )
        return tile, f[c, r] + total

    for t in range(SWEEPS):
        if t > 0:
            arrive(t)
        cols_in = (col_in[t, 0], col_in[t, 1])

        def sweep(r, cols):
            for c in range(COMPS):
                tile, total = flux(t, c, r, cols_in)
                fresh = (1.0 - RELAX) * tile + gain[r] * total
                v[t + 1, c, r + 1] = fresh
                cols = pack(t + 1, c * n_r + r, fresh, cols)
            return cols

        low, high = over_radius(sweep, no_cols)
        col_out[t + 1, 0] = low
        col_out[t + 1, 1] = high
        start(t + 1)

    final = v.at[SWEEPS]
    store_v = pltpu.make_async_copy(final.at[:, pl.ds(1, n_r)], newv, out_sem.at[0])
    store_v.start()

    def s1_copy(step):
        return pltpu.make_async_remote_copy(
            stage_out.at[0], lat_sums.at[me_lat], s1_send.at[step - 1], s1_recv.at[me_lat],
            device_id={"lat": lax.rem(me_lat + step, n_lat)}, device_id_type=MESH,
        )

    def s2_copy(step):
        return pltpu.make_async_remote_copy(
            stage_out.at[1], lon_sums.at[me_lon], s2_send.at[step - 1], s2_recv.at[me_lon],
            device_id={
                "lon": lax.rem(me_lon + step // n_rad, n_lon),
                "rad": lax.rem(me_rad + step % n_rad, n_rad),
            },
            device_id_type=MESH,
        )

    def received(buffer, sem, index):
        pltpu.make_async_remote_copy(
            stage_out.at[0], buffer.at[index], s1_send.at[0], sem.at[index],
            device_id={"lon": lon_up}, device_id_type=MESH,
        ).wait_recv()

    @pl.when(is_top)
    def _():
        drag = [eta[n_r] * (final[c, n_r] - final[c, n_r - 1]) for c in range(COMPS)]
        twist = (
            (ry * drag[2] - rz * drag[1]) * cos_lat,
            (rz * drag[0] - rx * drag[2]) * cos_lat,
            (rx * drag[1] - ry * drag[0]) * cos_lat,
            cos_lat,
        )
        packed = jnp.zeros((1, LANES), jnp.float32)
        for band in range(n_a // FACE):
            cut = slice(band * FACE, (band + 1) * FACE)
            rows = jnp.concatenate(
                [jnp.sum(x[cut], axis=0, keepdims=True) for x in twist]
                + [jnp.zeros((4, n_o), jnp.float32)], 0,
            )
            sums = lax.dot_general(
                rows, onehots[band], (((1,), (1,)), ((), ())), precision=HIGHEST,
                preferred_element_type=jnp.float32,
            )
            packed = packed + jnp.concatenate([sums[i : i + 1] for i in range(COMPS + 1)], 1)
        stage_out[0] = packed
        lat_sums[me_lat] = packed
        for step in range(1, n_lat):
            s1_copy(step).start()
        for step in range(1, n_lat):
            received(lat_sums, s1_recv, lax.rem(me_lat + step, n_lat))
        total = lat_sums[0]
        for i in range(1, n_lat):
            total = total + lat_sums[i]
        stage_out[1] = total
        lon_sums[me_lon] = total
        for step in range(1, n_lon * n_rad):
            s2_copy(step).start()

    arrive(SWEEPS)
    cols_in = (col_in[SWEEPS, 0], col_in[SWEEPS, 1])

    def remain(q, carry):
        for c in range(COMPS):
            two = jnp.zeros((n_a, n_o), jnp.float32)
            for s in range(2):
                r = 2 * q + s
                tile, total = flux(SWEEPS, c, r, cols_in)
                two = two + (total - diag[r] * tile)
            at = pl.ds(pl.multiple_of((c * (n_r // 2) + q) * n_a, n_a), n_a)
            for h in range(reps):
                pairs[h, at] = two[:, h * LANES : (h + 1) * LANES]
        return carry

    def remain_block(i, carry):
        for j in range(2):
            carry = remain(2 * i + j, carry)
        return carry

    lax.fori_loop(0, n_r // 4, remain_block, 0)
    half = n_o // 2
    thin_r = lax.broadcasted_iota(jnp.int32, (LANES, half), 0)
    thin_c = lax.broadcasted_iota(jnp.int32, (LANES, half), 1)
    count = COMPS * (n_r // 2) * n_a // 2
    merged = jnp.zeros((count, half), jnp.float32)
    for h in range(reps):
        pick = jnp.where((thin_r + h * LANES) // 2 == thin_c, 0.125, 0.0).astype(jnp.bfloat16)
        both = pairs[h, pl.ds(0, count, stride=2)] + pairs[h, pl.ds(1, count, stride=2)]
        big = both.astype(jnp.bfloat16)
        small = (both - big.astype(jnp.float32)).astype(jnp.bfloat16)
        merged = merged + (
            jnp.dot(big, pick, preferred_element_type=jnp.float32)
            + jnp.dot(small, pick, preferred_element_type=jnp.float32)
        )
    mine = count // COMPS
    spot = pl.ds(pl.multiple_of(me_rad * mine, mine), mine)
    for c in range(COMPS):
        coarse[c, spot] = merged[c * mine : (c + 1) * mine]

    def g_copy(step):
        return pltpu.make_async_remote_copy(
            coarse.at[:, spot], coarse.at[:, spot], g_send.at[step - 1], g_recv.at[me_rad],
            device_id={"rad": lax.rem(me_rad + step, n_rad)}, device_id_type=MESH,
        )

    for step in range(1, n_rad):
        g_copy(step).start()

    for i in range(n_lon):
        @pl.when(jnp.logical_or(jnp.logical_not(is_top), me_lon != i))
        def _():
            received(lon_sums, s2_recv, i)
    total = lon_sums[0]
    for i in range(1, n_lon):
        total = total + lon_sums[i]
    area = total[:, COMPS * SLOT : (COMPS + 1) * SLOT]
    valid = lax.broadcasted_iota(jnp.int32, (1, SLOT), 1) < PLATES
    root = jnp.sqrt(jnp.where(valid, area, 1.0))
    turns = jnp.concatenate(
        [total[:, i * SLOT : (i + 1) * SLOT] / root for i in range(COMPS)]
        + [jnp.zeros((8 - COMPS, SLOT), jnp.float32)], 0,
    )
    for band in range(n_a // FACE):
        cut = slice(band * FACE, (band + 1) * FACE)
        cell = jnp.dot(turns, onehots[band], precision=HIGHEST, preferred_element_type=jnp.float32)
        ox, oy, oz = (cell[i : i + 1] for i in range(COMPS))
        plate[0, cut] = oy * rz[cut] - oz * ry[cut]
        plate[1, cut] = oz * rx[cut] - ox * rz[cut]
        plate[2, cut] = ox * ry[cut] - oy * rx[cut]

    for t in range(SWEEPS + 1):
        sent(t)

    @pl.when(is_top)
    def _():
        for step in range(1, n_lat):
            s1_copy(step).wait_send()
        for step in range(1, n_lon * n_rad):
            s2_copy(step).wait_send()

    for step in range(1, n_rad):
        source = lax.rem(me_rad + step, n_rad)
        region = coarse.at[:, pl.ds(pl.multiple_of(source * mine, mine), mine)]
        pltpu.make_async_remote_copy(
            region, region, g_send.at[0], g_recv.at[source],
            device_id={"rad": source}, device_id_type=MESH,
        ).wait_recv()
        g_copy(step).wait_send()
    store_v.wait()


def on_device(sizes, velocity, forcing, viscosity, plate_ids):
    n_lat, n_lon, n_rad = sizes
    _, n_r, n_a, n_o = velocity.shape
    rounds = SWEEPS + 1
    f32 = jnp.float32
    dma = pltpu.SemaphoreType.DMA
    in_any = pl.BlockSpec(memory_space=pl.ANY)
    in_vmem = pl.BlockSpec(memory_space=pltpu.VMEM)
    coarse_rows = n_rad * (n_r // 2) * (n_a // 2)
    new_v, coarse, plate = pl.pallas_call(
        functools.partial(kernel, sizes),
        out_shape=(
            jax.ShapeDtypeStruct(velocity.shape, f32),
            jax.ShapeDtypeStruct((COMPS, coarse_rows, n_o // 2), f32),
            jax.ShapeDtypeStruct((COMPS, n_a, n_o), f32),
        ),
        in_specs=[in_any, in_any, in_any, in_vmem],
        out_specs=(in_any, in_vmem, in_vmem),
        scratch_shapes=[
            pltpu.VMEM((rounds, COMPS, n_r + 2, n_a, n_o), f32),
            pltpu.VMEM((COMPS, n_r, n_a, n_o), f32),
            pltpu.VMEM((n_r + 2, n_a, n_o), f32),
            pltpu.VMEM((2, n_r, n_a, n_o), f32),
            pltpu.VMEM((2, n_r, n_a, n_o), f32),
            pltpu.VMEM((n_r + 1, n_a, n_o), f32),
            pltpu.VMEM((n_r, n_a, n_o), f32),
            pltpu.VMEM((n_r, n_a, n_o), f32),
            pltpu.VMEM((rounds, 2, (COMPS + 1) * n_r, 1, n_o), f32),
            pltpu.VMEM((rounds, 2, (COMPS + 1) * n_r, 1, n_o), f32),
            pltpu.VMEM((rounds, 2, n_a, LANES), f32),
            pltpu.VMEM((rounds, 2, n_a, LANES), f32),
            pltpu.VMEM((n_o // LANES, COMPS * (n_r // 2) * n_a, LANES), f32),
            pltpu.VMEM((n_lat, 1, LANES), f32),
            pltpu.VMEM((n_lon, 1, LANES), f32),
            pltpu.VMEM((2, 1, LANES), f32),
            dma((3,)),
            dma((rounds, 8)),
            dma((rounds, 8)),
            dma((n_lat,)),
            dma((n_lat,)),
            dma((n_lon * n_rad,)),
            dma((n_lon,)),
            dma((n_rad,)),
            dma((n_rad,)),
            dma((1,)),
        ],
        compiler_params=pltpu.CompilerParams(collective_id=0, has_side_effects=True),
    )(velocity, forcing, viscosity, plate_ids)
    coarse = coarse.reshape(COMPS, n_rad * (n_r // 2), n_a // 2, n_o // 2)
    return new_v, coarse, plate


def solution(mesh):
    sizes = tuple(mesh.shape[a] for a in ("lat", "lon", "rad"))
    field = P(None, "rad", "lat", "lon")
    return jax.shard_map(
        functools.partial(on_device, sizes),
        mesh=mesh,
        in_specs=(field, field, P("rad", "lat", "lon"), P("lat", "lon")),
        out_specs=(field, P(None, None, "lat", "lon"), P(None, "lat", "lon")),
        check_vma=False,
    )
```

time: 162 us -> 29.1 us (0.18)
  blocking collectives: 42.5 us -> 0 us
  waiting for transfers between devices: 34.2 us -> 0 us
  other arithmetic: 32.6 us -> 0 us
  local copies, waits for them, and re-layouts: 34 us -> 3.15 us
  Pallas kernels: 0 us -> 25.1 us
  starting transfers between devices: 16.8 us -> 0 us
    psum x1 -> x0, blocking collectives: 40.6 us -> none  [on_device(): sums = lax.psum(partial_sums, ('lat', 'lon', 'rad'))]
    ppermute x6 -> x0, waiting for transfers between devices: 34.2 us -> none  [the longest x3 19.9 us: padded(): lax.ppermute(lax.slice_in_dim(block, 0, width, axis=dim), axis, backward)]
    reshape x1 -> x0, local copies, waits for them, and re-layouts: 26.5 us -> none  [restrict(): residual_field.reshape(shape_all[0], shape_all[1] // 2, 2, shape_all[2] /...]
    pallas_call x0 -> x1, Pallas kernels: none -> 25.1 us  [on_device(): pl.pallas_call(functools.partial(kernel, sizes), out_shape=(jax.ShapeDtyp...]
    ppermute x6 -> x0, starting transfers between devices: 16.8 us -> none  [the longest x3 13.2 us: padded(): lax.ppermute(lax.slice_in_dim(block, block.shape[dim] - width, None, axis...]
    select_n x6 -> x0, other arithmetic: 13.6 us -> none  [the longest x3 10.1 us: relax_step(): return jnp.where(inside, updated, center_vel)]
    reduce_sum x1 -> x0, other arithmetic: 9.42 us -> none  [restrict(): return jnp.mean(blocks, axis=(2, 4, 6))]
    concatenate x3 -> x0, other arithmetic: 7.04 us -> none  [the longest x2 5.72 us: padded(): block = jnp.concatenate([low, block, high], axis=dim)]
  transfers between devices with their start and end apart: 6 -> 0, of which waited for: 5 -> 0; matrix products, arithmetic and copies ran while one was open for 1% -> 0% of each run, Pallas kernels for 0% -> 0%
where the time goes in v1:
time: 29.1 us; the launch traced here: 28.9 us
  Pallas kernels  25.1 us (86%)
  local copies, waits for them, and re-layouts  3.15 us (11%)
  between operations  0.65 us (2%)
    pallas_call x1, Pallas kernels, on_device(): pl.pallas_call(functools.partial(kernel, sizes), out_shape=(jax.ShapeDtyp...  25.1 us
    unnamed x7, local copies, waits for them, and re-layouts  3.15 us

profile of v1, /device:TPU:0, one launch (start us, length us, event | category | flops | bytes accessed | tf_op | source)
XLA Modules:
  0.0 28.9 jit_solution(6069805617092083980)
XLA Ops:
  0.6 25.1 %shard_map.67 = (f32[3,16,8,256]{3,2,1,0:T(8,128)}, f32[3,64,128]{2,1,0:T(8,128)}, f32[3,8,256]{2,1,0:T(8,128)}) custom-call(f32[3,16,8,256]{3,2,1,0:T(8,128)} %vel.1, f32[3,16,8,256]{3,2,1,0:T(8,128)} %forc.1, f32[16,8,256]{2,1,0:T(8,128)} %visc.1, s32[1,32]{1,0:T(1,128)} %ids.1), custom_call_target="tpu_custom_call" | custom-call | tf_op jit(solution)/shard_map/pallas_call | solution.py:414
  25.7 0.0 copy-start
  25.7 1.8 %copy.10 = f32[3,16,8,256]{3,2,1,0:T(8,128)} copy(f32[3,16,8,256]{3,2,1,0:T(8,128)} %get-tuple-element.12) | data formatting | bytes 786432
  27.6 0.0 copy-done
  27.6 0.0 copy-start.1
  27.6 0.6 %copy.11 = f32[3,16,4,128]{3,2,1,0:T(4,128)} copy(f32[3,16,4,128]{3,2,1,0:T(4,128)S(1)} %bitcast.1) | data formatting | bytes 196608
  28.2 0.1 copy-done.1
  28.3 0.6 %copy.12 = f32[3,8,256]{2,1,0:T(8,128)} copy(f32[3,8,256]{2,1,0:T(8,128)S(1)} %copy-done.1) | data formatting | bytes 49152
Async XLA Ops:
  25.7 1.8 %copy-start = (f32[3,64,128]{2,1,0:T(8,128)S(1)}, f32[3,64,128]{2,1,0:T(8,128)}, u32[]{:S(2)}) copy-start(f32[3,64,128]{2,1,0:T(8,128)} %get-tuple-element.7) | copy-start | bytes 294916
  27.6 0.7 %copy-start.1 = (f32[3,8,256]{2,1,0:T(8,128)S(1)}, f32[3,8,256]{2,1,0:T(8,128)}, u32[]{:S(2)}) copy-start(f32[3,8,256]{2,1,0:T(8,128)} %get-tuple-element.14) | copy-start | bytes 73732

commit v2 on v1

--- a/solution.py
+++ b/solution.py
@@ -25,12 +25,12 @@
 
 
 def kernel(
-    sizes, vel, forc, visc, ids,
-    newv, coarse, plate,
-    v, f, eta, w_lat, w_lon, w_rad, gain, diag,
+    sizes, vel, forc, visc, ids_in,
+    last, coarse, plate,
+    early, ids, f, eta, w_lat, w_lon, w_rad, gain, diag,
     face_out, face_in, col_out, col_in, pairs,
     lat_sums, lon_sums, stage_out,
-    load_sem, send_sem, recv_sem, s1_send, s1_recv, s2_send, s2_recv, g_send, g_recv, out_sem,
+    load_sem, send_sem, recv_sem, s1_send, s1_recv, s2_send, s2_recv, g_send, g_recv,
 ):
     n_lat, n_lon, n_rad = sizes
     n_r, n_a, n_o = visc.shape
@@ -39,11 +39,13 @@
     rad_lo, rad_hi = me_rad > 0, me_rad < n_rad - 1
     lon_up, lon_dn = lax.rem(me_lon + 1, n_lon), lax.rem(me_lon + n_lon - 1, n_lon)
     is_top = me_rad == n_rad - 1
+    v = [early.at[t] for t in range(SWEEPS)] + [last]
 
     loads = [
         pltpu.make_async_copy(visc, eta.at[pl.ds(1, n_r)], load_sem.at[0]),
-        pltpu.make_async_copy(vel, v.at[0, :, pl.ds(1, n_r)], load_sem.at[1]),
+        pltpu.make_async_copy(vel, v[0].at[:, pl.ds(1, n_r)], load_sem.at[1]),
         pltpu.make_async_copy(forc, f, load_sem.at[2]),
+        pltpu.make_async_copy(ids_in, ids, load_sem.at[3]),
     ]
     for load in loads:
         load.start()
@@ -86,7 +88,7 @@
             eta[slot] = zero_plane
             for t in range(SWEEPS + 1):
                 for c in range(COMPS):
-                    v[t, c, slot] = zero_plane
+                    v[t][c, slot] = zero_plane
     for has, side in ((lat_lo, 0), (lat_hi, 1)):
         @pl.when(jnp.logical_not(has))
         def _():
@@ -106,8 +108,8 @@
             (remote(face_out.at[t, 0, rows], face_in.at[t, 1, rows], 1, {"lat": me_lat - 1}), lat_lo, lat_hi),
             (remote(col_out.at[t, 1], col_in.at[t, 0], 2, {"lon": lon_up}), None, None),
             (remote(col_out.at[t, 0], col_in.at[t, 1], 3, {"lon": lon_dn}), None, None),
-            (remote(v.at[t, :, n_r], v.at[t, :, 0], 4, {"rad": me_rad + 1}), rad_hi, rad_lo),
-            (remote(v.at[t, :, 1], v.at[t, :, n_r + 1], 5, {"rad": me_rad - 1}), rad_lo, rad_hi),
+            (remote(v[t].at[:, n_r], v[t].at[:, 0], 4, {"rad": me_rad + 1}), rad_hi, rad_lo),
+            (remote(v[t].at[:, 1], v[t].at[:, n_r + 1], 5, {"rad": me_rad - 1}), rad_lo, rad_hi),
         ]
         if t == 0:
             out += [
@@ -143,13 +145,18 @@
         high = jnp.where(hit, pltpu.roll(tile[:, n_o - LANES :], lax.rem(k + 1, LANES), 1), high)
         return low, high
 
-    def over_radius(body, init):
+    def over_radius(body, init, after_top=None):
         def block(i, carry):
             for j in range(UNROLL):
                 carry = body(i * UNROLL + j, carry)
             return carry
 
-        return lax.fori_loop(0, n_r // UNROLL, block, init)
+        count = n_r // UNROLL
+        if after_top is not None:
+            count = count - 1
+            init = block(count, init)
+            after_top()
+        return lax.fori_loop(0, count, block, init)
 
     no_cols = (jnp.zeros((n_a, LANES), jnp.float32),) * 2
 
@@ -170,7 +177,7 @@
 
     def pack_first(r, cols):
         for c in range(COMPS):
-            cols = pack(0, c * n_r + r, v[0, c, r + 1], cols)
+            cols = pack(0, c * n_r + r, v[0][c, r + 1], cols)
         return pack(0, COMPS * n_r + r, eta[r + 1], cols)
 
     low, high = over_radius(pack_first, no_cols)
@@ -179,6 +186,7 @@
     pl.semaphore_wait(barrier, expected)
     start(0)
 
+    loads[3].wait()
     lat_cell = (me_lat * n_a + row).astype(jnp.float32)
     lon_cell = (me_lon * n_o + lane_wide).astype(jnp.float32)
     phi = math.pi * ((lat_cell + 0.5) / (n_lat * n_a) - 0.5)
@@ -222,36 +230,14 @@
     loads[2].wait()
 
     def flux(t, c, r, cols):
-        tile = v[t, c, r + 1]
+        tile = v[t][c, r + 1]
         below, above, west, east = shifted(t, c * n_r + r, tile, cols)
         total = (
             (w_lat[0, r] * below + w_lat[1, r] * above)
             + (w_lon[0, r] * west + w_lon[1, r] * east)
-            + (w_rad[r] * v[t, c, r] + w_rad[r + 1] * v[t, c, r + 2])
+            + (w_rad[r] * v[t][c, r] + w_rad[r + 1] * v[t][c, r + 2])
         )
         return tile, f[c, r] + total
-
-    for t in range(SWEEPS):
-        if t > 0:
-            arrive(t)
-        cols_in = (col_in[t, 0], col_in[t, 1])
-
-        def sweep(r, cols):
-            for c in range(COMPS):
-                tile, total = flux(t, c, r, cols_in)
-                fresh = (1.0 - RELAX) * tile + gain[r] * total
-                v[t + 1, c, r + 1] = fresh
-                cols = pack(t + 1, c * n_r + r, fresh, cols)
-            return cols
-
-        low, high = over_radius(sweep, no_cols)
-        col_out[t + 1, 0] = low
-        col_out[t + 1, 1] = high
-        start(t + 1)
-
-    final = v.at[SWEEPS]
-    store_v = pltpu.make_async_copy(final.at[:, pl.ds(1, n_r)], newv, out_sem.at[0])
-    store_v.start()
 
     def s1_copy(step):
         return pltpu.make_async_remote_copy(
@@ -275,9 +261,8 @@
             device_id={"lon": lon_up}, device_id_type=MESH,
         ).wait_recv()
 
-    @pl.when(is_top)
-    def _():
-        drag = [eta[n_r] * (final[c, n_r] - final[c, n_r - 1]) for c in range(COMPS)]
+    def torques():
+        drag = [eta[n_r] * (last[c, n_r] - last[c, n_r - 1]) for c in range(COMPS)]
         twist = (
             (ry * drag[2] - rz * drag[1]) * cos_lat,
             (rz * drag[0] - rx * drag[2]) * cos_lat,
@@ -300,6 +285,28 @@
         lat_sums[me_lat] = packed
         for step in range(1, n_lat):
             s1_copy(step).start()
+
+    for t in range(SWEEPS):
+        if t > 0:
+            arrive(t)
+        cols_in = (col_in[t, 0], col_in[t, 1])
+
+        def sweep(r, cols):
+            for c in range(COMPS):
+                tile, total = flux(t, c, r, cols_in)
+                fresh = (1.0 - RELAX) * tile + gain[r] * total
+                v[t + 1][c, r + 1] = fresh
+                cols = pack(t + 1, c * n_r + r, fresh, cols)
+            return cols
+
+        after_top = (lambda: pl.when(is_top)(torques)) if t == SWEEPS - 1 else None
+        low, high = over_radius(sweep, no_cols, after_top)
+        col_out[t + 1, 0] = low
+        col_out[t + 1, 1] = high
+        start(t + 1)
+
+    @pl.when(is_top)
+    def _():
         for step in range(1, n_lat):
             received(lat_sums, s1_recv, lax.rem(me_lat + step, n_lat))
         total = lat_sums[0]
@@ -399,7 +406,19 @@
             device_id={"rad": source}, device_id_type=MESH,
         ).wait_recv()
         g_copy(step).wait_send()
-    store_v.wait()
+
+
+def write_out(last, coarse, plate, new_v_out, coarse_out, plate_out, sem):
+    n_r = new_v_out.shape[1]
+    copies = [
+        pltpu.make_async_copy(last.at[:, pl.ds(1, n_r)], new_v_out, sem.at[0]),
+        pltpu.make_async_copy(coarse, coarse_out, sem.at[1]),
+        pltpu.make_async_copy(plate, plate_out, sem.at[2]),
+    ]
+    for copy in copies:
+        copy.start()
+    for copy in copies:
+        copy.wait()
 
 
 def on_device(sizes, velocity, forcing, viscosity, plate_ids):
@@ -411,17 +430,18 @@
     in_any = pl.BlockSpec(memory_space=pl.ANY)
     in_vmem = pl.BlockSpec(memory_space=pltpu.VMEM)
     coarse_rows = n_rad * (n_r // 2) * (n_a // 2)
-    new_v, coarse, plate = pl.pallas_call(
+    held = pl.pallas_call(
         functools.partial(kernel, sizes),
         out_shape=(
-            jax.ShapeDtypeStruct(velocity.shape, f32),
-            jax.ShapeDtypeStruct((COMPS, coarse_rows, n_o // 2), f32),
-            jax.ShapeDtypeStruct((COMPS, n_a, n_o), f32),
+            pltpu.VMEM((COMPS, n_r + 2, n_a, n_o), f32),
+            pltpu.VMEM((COMPS, coarse_rows, n_o // 2), f32),
+            pltpu.VMEM((COMPS, n_a, n_o), f32),
         ),
-        in_specs=[in_any, in_any, in_any, in_vmem],
-        out_specs=(in_any, in_vmem, in_vmem),
+        in_specs=[pl.BlockSpec(memory_space=pltpu.HBM)] * 4,
+        out_specs=(in_vmem,) * 3,
         scratch_shapes=[
-            pltpu.VMEM((rounds, COMPS, n_r + 2, n_a, n_o), f32),
+            pltpu.VMEM((SWEEPS, COMPS, n_r + 2, n_a, n_o), f32),
+            pltpu.VMEM(plate_ids.shape, jnp.int32),
             pltpu.VMEM((COMPS, n_r, n_a, n_o), f32),
             pltpu.VMEM((n_r + 2, n_a, n_o), f32),
             pltpu.VMEM((2, n_r, n_a, n_o), f32),
@@ -437,7 +457,7 @@
             pltpu.VMEM((n_lat, 1, LANES), f32),
             pltpu.VMEM((n_lon, 1, LANES), f32),
             pltpu.VMEM((2, 1, LANES), f32),
-            dma((3,)),
+            dma((4,)),
             dma((rounds, 8)),
             dma((rounds, 8)),
             dma((n_lat,)),
@@ -446,10 +466,26 @@
             dma((n_lon,)),
             dma((n_rad,)),
             dma((n_rad,)),
-            dma((1,)),
         ],
-        compiler_params=pltpu.CompilerParams(collective_id=0, has_side_effects=True),
-    )(velocity, forcing, viscosity, plate_ids)
+        compiler_params=pltpu.CompilerParams(
+            collective_id=0, has_side_effects=True, vmem_limit_bytes=24 * 2**20
+        ),
+    )(*(
+        pltpu.with_memory_space_constraint(x, pltpu.HBM)
+        for x in (velocity, forcing, viscosity, plate_ids)
+    ))
+    new_v, coarse, plate = pl.pallas_call(
+        write_out,
+        out_shape=(
+            jax.ShapeDtypeStruct(velocity.shape, f32),
+            jax.ShapeDtypeStruct((COMPS, coarse_rows, n_o // 2), f32),
+            jax.ShapeDtypeStruct((COMPS, n_a, n_o), f32),
+        ),
+        in_specs=[in_vmem] * 3,
+        out_specs=(in_any,) * 3,
+        scratch_shapes=[dma((3,))],
+        compiler_params=pltpu.CompilerParams(vmem_limit_bytes=4 * 2**20),
+    )(*(pltpu.with_memory_space_constraint(x, pltpu.VMEM) for x in held))
     coarse = coarse.reshape(COMPS, n_rad * (n_r // 2), n_a // 2, n_o // 2)
     return new_v, coarse, plate
 

time: 29.1 us -> 25.4 us (0.87)
  local copies, waits for them, and re-layouts: 3.15 us -> 0 us
  Pallas kernels: 25.1 us -> 24.7 us
    unnamed x7 -> x0, local copies, waits for them, and re-layouts: 3.15 us -> none
    pallas_call x1 -> x2, Pallas kernels: 25.1 us -> 24.7 us  [the longest x1 23.9 us: on_device(): pl.pallas_call(functools.partial(kernel, sizes), out_shape=(pltpu.VMEM((C...]
where the time goes in v2:
time: 25.4 us; the launch traced here: 25.3 us
  Pallas kernels  24.7 us (97%)
  between operations  0.64 us (3%)
    pallas_call x1, Pallas kernels, on_device(): pl.pallas_call(functools.partial(kernel, sizes), out_shape=(pltpu.VMEM((C...  23.9 us
    pallas_call x1, Pallas kernels, on_device(): pl.pallas_call(write_out, out_shape=(jax.ShapeDtypeStruct(velocity.shape,...  0.8 us

profile of v2, /device:TPU:0, one launch (start us, length us, event | category | flops | bytes accessed | tf_op | source)
XLA Modules:
  0.0 25.3 jit_solution(9092093473648521894)
XLA Ops:
  0.6 23.9 %shard_map.67 = (f32[3,18,8,256]{3,2,1,0:T(8,128)S(1)}, f32[3,64,128]{2,1,0:T(8,128)S(1)}, f32[3,8,256]{2,1,0:T(8,128)S(1)}) custom-call(f32[3,16,8,256]{3,2,1,0:T(8,128)} %vel.1, f32[3,16,8,256]{3,2,1,0:T(8,128)} %forc.1, f32[16,8,256]{2,1,0:T(8,128)} %visc.1, s32[1,32]{1,0:T(1,128)} %ids_in.1), custom_call_target="tpu_custom_call" | custom-call | tf_op jit(solution)/shard_map/pallas_call | solution.py:433
  24.5 0.8 %shard_map.68 = (f32[3,16,8,256]{3,2,1,0:T(8,128)}, f32[3,64,128]{2,1,0:T(8,128)}, f32[3,8,256]{2,1,0:T(8,128)}) custom-call(f32[3,18,8,256]{3,2,1,0:T(8,128)S(1)} %get-tuple-element.9.last, f32[3,64,128]{2,1,0:T(8,128)S(1)} %get-tuple-element.10.coarse, f32[3,8,256]{2,1,0:T(8,128)S(1)} %get-tuple-element.11.plate), custom_call_target="tpu_custom_call" | custom-call | tf_op jit(solution)/shard_map/pallas_call | solution.py:477

commit v3 on v2

--- a/solution.py
+++ b/solution.py
@@ -22,6 +22,20 @@
 
 def harmonic(own, other):
     return 2.0 * own * other / (own + other)
+
+
+class Link:
+    def __init__(self, make):
+        self.make = make
+
+    def start(self):
+        self.make().start()
+
+    def wait_send(self):
+        self.make().wait_send()
+
+    def wait_recv(self):
+        self.make().wait_recv()
 
 
 def kernel(
@@ -40,15 +54,6 @@
     lon_up, lon_dn = lax.rem(me_lon + 1, n_lon), lax.rem(me_lon + n_lon - 1, n_lon)
     is_top = me_rad == n_rad - 1
     v = [early.at[t] for t in range(SWEEPS)] + [last]
-
-    loads = [
-        pltpu.make_async_copy(visc, eta.at[pl.ds(1, n_r)], load_sem.at[0]),
-        pltpu.make_async_copy(vel, v[0].at[:, pl.ds(1, n_r)], load_sem.at[1]),
-        pltpu.make_async_copy(forc, f, load_sem.at[2]),
-        pltpu.make_async_copy(ids_in, ids, load_sem.at[3]),
-    ]
-    for load in loads:
-        load.start()
 
     barrier = pltpu.get_barrier_semaphore()
 
@@ -76,6 +81,15 @@
             })
         expected = expected + (n_lon * n_rad - 1)
 
+    loads = [
+        pltpu.make_async_copy(visc, eta.at[pl.ds(1, n_r)], load_sem.at[0]),
+        pltpu.make_async_copy(vel, v[0].at[:, pl.ds(1, n_r)], load_sem.at[1]),
+        pltpu.make_async_copy(forc, f, load_sem.at[2]),
+        pltpu.make_async_copy(ids_in, ids, load_sem.at[3]),
+    ]
+    for load in loads:
+        load.start()
+
     lane_wide = lax.broadcasted_iota(jnp.int32, (n_a, n_o), 1)
     lane = lax.broadcasted_iota(jnp.int32, (n_a, LANES), 1)
     row = lax.broadcasted_iota(jnp.int32, (n_a, n_o), 0)
@@ -95,28 +109,33 @@
             for t in range(SWEEPS + 1):
                 face_in[t, side] = jnp.zeros(face_in.shape[2:], jnp.float32)
 
-    def links(t):
-        rows = pl.ds(0, ((COMPS + 1) if t == 0 else COMPS) * n_r)
+    blocks_r = n_r // UNROLL
+    order = [blocks_r - 1] + list(range(blocks_r - 1))
+
+    def chunk(t, b):
+        comps = COMPS + 1 if t == 0 else COMPS
+        rows = pl.ds(b * UNROLL * comps, UNROLL * comps)
 
         def remote(src, dst, k, device):
-            return pltpu.make_async_remote_copy(
-                src, dst, send_sem.at[t, k], recv_sem.at[t, k], device_id=device, device_id_type=MESH
-            )
-
-        out = [
-            (remote(face_out.at[t, 1, rows], face_in.at[t, 0, rows], 0, {"lat": me_lat + 1}), lat_hi, lat_lo),
-            (remote(face_out.at[t, 0, rows], face_in.at[t, 1, rows], 1, {"lat": me_lat - 1}), lat_lo, lat_hi),
-            (remote(col_out.at[t, 1], col_in.at[t, 0], 2, {"lon": lon_up}), None, None),
-            (remote(col_out.at[t, 0], col_in.at[t, 1], 3, {"lon": lon_dn}), None, None),
-            (remote(v[t].at[:, n_r], v[t].at[:, 0], 4, {"rad": me_rad + 1}), rad_hi, rad_lo),
-            (remote(v[t].at[:, 1], v[t].at[:, n_r + 1], 5, {"rad": me_rad - 1}), rad_lo, rad_hi),
+            return Link(functools.partial(
+                pltpu.make_async_remote_copy,
+                src, dst, send_sem.at[t, b, k], recv_sem.at[t, b, k],
+                device_id=device, device_id_type=MESH,
+            ))
+
+        sends = [
+            (remote(col_out.at[t, b, 1], col_in.at[t, b, 0], 2, {"lon": lon_up}), None),
+            (remote(col_out.at[t, b, 0], col_in.at[t, b, 1], 3, {"lon": lon_dn}), None),
+            (remote(face_out.at[t, 1, rows], face_in.at[t, 0, rows], 0, {"lat": me_lat + 1}), lat_hi),
+            (remote(face_out.at[t, 0, rows], face_in.at[t, 1, rows], 1, {"lat": me_lat - 1}), lat_lo),
         ]
+        takes = [None, None, lat_lo, lat_hi]
+        ups = [(remote(v[t].at[:, n_r], v[t].at[:, 0], 4, {"rad": me_rad + 1}), rad_hi)]
+        downs = [(remote(v[t].at[:, 1], v[t].at[:, n_r + 1], 5, {"rad": me_rad - 1}), rad_lo)]
         if t == 0:
-            out += [
-                (remote(eta.at[n_r], eta.at[0], 6, {"rad": me_rad + 1}), rad_hi, rad_lo),
-                (remote(eta.at[1], eta.at[n_r + 1], 7, {"rad": me_rad - 1}), rad_lo, rad_hi),
-            ]
-        return out
+            ups.append((remote(eta.at[n_r], eta.at[0], 6, {"rad": me_rad + 1}), rad_hi))
+            downs.append((remote(eta.at[1], eta.at[n_r + 1], 7, {"rad": me_rad - 1}), rad_lo))
+        return sends, takes, ups, downs
 
     def guarded(cond, call):
         if cond is None:
@@ -124,47 +143,65 @@
         else:
             pl.when(cond)(call)
 
-    def start(t):
-        for copy, sends, _ in links(t):
-            guarded(sends, copy.start)
-
-    def arrive(t):
-        for copy, _, receives in links(t):
-            guarded(receives, copy.wait_recv)
+    def start(t, b):
+        sends, _, _, _ = chunk(t, b)
+        for copy, cond in sends:
+            guarded(cond, copy.start)
+        if b == blocks_r - 1:
+            for copy, cond in chunk(t, 0)[2]:
+                guarded(cond, copy.start)
+        if b == 0:
+            for copy, cond in chunk(t, 0)[3]:
+                guarded(cond, copy.start)
+
+    def arrive(t, b):
+        sends, takes, _, _ = chunk(t, b)
+        _, _, ups, downs = chunk(t, 0)
+        if b == 0:
+            for copy, _ in ups:
+                guarded(rad_lo, copy.wait_recv)
+        if b == blocks_r - 1:
+            for copy, _ in downs:
+                guarded(rad_hi, copy.wait_recv)
+        for (copy, _), cond in zip(sends, takes):
+            guarded(cond, copy.wait_recv)
 
     def sent(t):
-        for copy, sends, _ in links(t):
-            guarded(sends, copy.wait_send)
-
-    def pack(t, k, tile, cols):
-        face_out[t, 0, k] = tile[:1]
-        face_out[t, 1, k] = tile[n_a - 1 :]
+        for b in range(blocks_r):
+            for copy, cond in chunk(t, b)[0]:
+                guarded(cond, copy.wait_send)
+        _, _, ups, downs = chunk(t, 0)
+        for copy, cond in ups + downs:
+            guarded(cond, copy.wait_send)
+
+    def lane_of(t, j, c):
+        return j * (COMPS + 1 if t == 0 else COMPS) + c
+
+    def row_of(t, r, c):
+        return r * (COMPS + 1 if t == 0 else COMPS) + c
+
+    def pack(t, b, j, c, tile, cols):
+        face_out[t, 0, row_of(t, b * UNROLL + j, c)] = tile[:1]
+        face_out[t, 1, row_of(t, b * UNROLL + j, c)] = tile[n_a - 1 :]
+        k = lane_of(t, j, c)
         low, high = cols
         hit = lane == k
-        low = jnp.where(hit, pltpu.roll(tile[:, :LANES], k, 1), low)
-        high = jnp.where(hit, pltpu.roll(tile[:, n_o - LANES :], lax.rem(k + 1, LANES), 1), high)
+        low = jnp.where(hit, pltpu.roll(tile[:, :LANES], k, 1) if k else tile[:, :LANES], low)
+        high = jnp.where(hit, pltpu.roll(tile[:, n_o - LANES :], (k + 1) % LANES, 1), high)
         return low, high
 
-    def over_radius(body, init, after_top=None):
-        def block(i, carry):
-            for j in range(UNROLL):
-                carry = body(i * UNROLL + j, carry)
-            return carry
-
-        count = n_r // UNROLL
-        if after_top is not None:
-            count = count - 1
-            init = block(count, init)
-            after_top()
-        return lax.fori_loop(0, count, block, init)
+    def put_cols(t, b, cols):
+        col_out[t, b, 0], col_out[t, b, 1] = cols
 
     no_cols = (jnp.zeros((n_a, LANES), jnp.float32),) * 2
 
-    def shifted(t, k, tile, cols):
+    def shifted(t, b, j, c, tile, cols):
         col_lo, col_hi = cols
-        below = jnp.where(row == 0, face_in[t, 0, k], pltpu.roll(tile, 1, 0))
-        above = jnp.where(row == n_a - 1, face_in[t, 1, k], pltpu.roll(tile, n_a - 1, 0))
-        from_lo = pltpu.roll(col_lo, lax.rem(LANES - k, LANES), 1)
+        k = lane_of(t, j, c)
+        at = row_of(t, b * UNROLL + j, c)
+        below = jnp.where(row == 0, face_in[t, 0, at], pltpu.roll(tile, 1, 0))
+        above = jnp.where(row == n_a - 1, face_in[t, 1, at], pltpu.roll(tile, n_a - 1, 0))
+        from_lo = pltpu.roll(col_lo, LANES - k, 1) if k else col_lo
         from_hi = pltpu.roll(col_hi, LANES - 1 - k, 1)
         west = jnp.where(lane_wide == 0, jnp.concatenate([from_lo] * reps, 1), pltpu.roll(tile, 1, 1))
         east = jnp.where(
@@ -174,17 +211,17 @@
 
     loads[0].wait()
     loads[1].wait()
-
-    def pack_first(r, cols):
-        for c in range(COMPS):
-            cols = pack(0, c * n_r + r, v[0][c, r + 1], cols)
-        return pack(0, COMPS * n_r + r, eta[r + 1], cols)
-
-    low, high = over_radius(pack_first, no_cols)
-    col_out[0, 0] = low
-    col_out[0, 1] = high
+    for b in order:
+        cols = no_cols
+        for j in range(UNROLL):
+            r = b * UNROLL + j
+            for c in range(COMPS):
+                cols = pack(0, b, j, c, v[0][c, r + 1], cols)
+            cols = pack(0, b, j, COMPS, eta[r + 1], cols)
+        put_cols(0, b, cols)
     pl.semaphore_wait(barrier, expected)
-    start(0)
+    for b in order:
+        start(0, b)
 
     loads[3].wait()
     lat_cell = (me_lat * n_a + row).astype(jnp.float32)
@@ -206,32 +243,28 @@
         cells = jnp.dot(own, spread, precision=HIGHEST)[:1]
         onehots.append((jnp.abs(cells - numbers.astype(jnp.float32)) < 0.5).astype(jnp.float32))
 
-    arrive(0)
-
-    cols_first = (col_in[0, 0], col_in[0, 1])
-    w_rad[0] = harmonic(eta[1], eta[0])
-
-    def weigh(r, carry):
-        own = eta[r + 1]
-        near = shifted(0, COMPS * n_r + r, own, cols_first)
-        below, above, west, east = (harmonic(own, other) for other in near)
-        up = harmonic(own, eta[r + 2])
-        w_lat[0, r] = below
-        w_lat[1, r] = above
-        w_lon[0, r] = west
-        w_lon[1, r] = east
-        w_rad[r + 1] = up
-        d = 0.5 * own + (below + above) + (west + east) + (up + w_rad[r])
-        diag[r] = d
-        gain[r] = RELAX / d
-        return carry
-
-    over_radius(weigh, 0)
-    loads[2].wait()
-
-    def flux(t, c, r, cols):
+    def weigh(b, cols):
+        for j in range(UNROLL):
+            r = b * UNROLL + j
+            own = eta[r + 1]
+            near = shifted(0, b, j, COMPS, own, cols)
+            below, above, west, east = (harmonic(own, other) for other in near)
+            down = harmonic(own, eta[r]) if j == 0 else up
+            up = harmonic(own, eta[r + 2])
+            w_lat[0, r] = below
+            w_lat[1, r] = above
+            w_lon[0, r] = west
+            w_lon[1, r] = east
+            w_rad[r] = down
+            w_rad[r + 1] = up
+            d = 0.5 * own + (below + above) + (west + east) + (up + down)
+            diag[r] = d
+            gain[r] = RELAX / d
+
+    def flux(t, b, j, c, cols):
+        r = b * UNROLL + j
         tile = v[t][c, r + 1]
-        below, above, west, east = shifted(t, c * n_r + r, tile, cols)
+        below, above, west, east = shifted(t, b, j, c, tile, cols)
         total = (
             (w_lat[0, r] * below + w_lat[1, r] * above)
             + (w_lon[0, r] * west + w_lon[1, r] * east)
@@ -287,23 +320,25 @@
             s1_copy(step).start()
 
     for t in range(SWEEPS):
-        if t > 0:
-            arrive(t)
-        cols_in = (col_in[t, 0], col_in[t, 1])
-
-        def sweep(r, cols):
-            for c in range(COMPS):
-                tile, total = flux(t, c, r, cols_in)
-                fresh = (1.0 - RELAX) * tile + gain[r] * total
-                v[t + 1][c, r + 1] = fresh
-                cols = pack(t + 1, c * n_r + r, fresh, cols)
-            return cols
-
-        after_top = (lambda: pl.when(is_top)(torques)) if t == SWEEPS - 1 else None
-        low, high = over_radius(sweep, no_cols, after_top)
-        col_out[t + 1, 0] = low
-        col_out[t + 1, 1] = high
-        start(t + 1)
+        for b in order:
+            arrive(t, b)
+            cols_in = (col_in[t, b, 0], col_in[t, b, 1])
+            if t == 0:
+                weigh(b, cols_in)
+                if b == order[0]:
+                    loads[2].wait()
+            cols = no_cols
+            for j in range(UNROLL):
+                r = b * UNROLL + j
+                for c in range(COMPS):
+                    tile, total = flux(t, b, j, c, cols_in)
+                    fresh = (1.0 - RELAX) * tile + gain[r] * total
+                    v[t + 1][c, r + 1] = fresh
+                    cols = pack(t + 1, b, j, c, fresh, cols)
+            put_cols(t + 1, b, cols)
+            if t == SWEEPS - 1 and b == blocks_r - 1:
+                pl.when(is_top)(torques)
+            start(t + 1, b)
 
     @pl.when(is_top)
     def _():
@@ -317,27 +352,18 @@
         for step in range(1, n_lon * n_rad):
             s2_copy(step).start()
 
-    arrive(SWEEPS)
-    cols_in = (col_in[SWEEPS, 0], col_in[SWEEPS, 1])
-
-    def remain(q, carry):
-        for c in range(COMPS):
-            two = jnp.zeros((n_a, n_o), jnp.float32)
-            for s in range(2):
-                r = 2 * q + s
-                tile, total = flux(SWEEPS, c, r, cols_in)
-                two = two + (total - diag[r] * tile)
-            at = pl.ds(pl.multiple_of((c * (n_r // 2) + q) * n_a, n_a), n_a)
-            for h in range(reps):
-                pairs[h, at] = two[:, h * LANES : (h + 1) * LANES]
-        return carry
-
-    def remain_block(i, carry):
-        for j in range(2):
-            carry = remain(2 * i + j, carry)
-        return carry
-
-    lax.fori_loop(0, n_r // 4, remain_block, 0)
+    for b in order:
+        arrive(SWEEPS, b)
+        cols_in = (col_in[SWEEPS, b, 0], col_in[SWEEPS, b, 1])
+        for i in range(UNROLL // 2):
+            for c in range(COMPS):
+                two = jnp.zeros((n_a, n_o), jnp.float32)
+                for j in (2 * i, 2 * i + 1):
+                    tile, total = flux(SWEEPS, b, j, c, cols_in)
+                    two = two + (total - diag[b * UNROLL + j] * tile)
+                at = pl.ds((c * (n_r // 2) + b * (UNROLL // 2) + i) * n_a, n_a)
+                for h in range(reps):
+                    pairs[h, at] = two[:, h * LANES : (h + 1) * LANES]
     half = n_o // 2
     thin_r = lax.broadcasted_iota(jnp.int32, (LANES, half), 0)
     thin_c = lax.broadcasted_iota(jnp.int32, (LANES, half), 1)
@@ -425,6 +451,7 @@
     n_lat, n_lon, n_rad = sizes
     _, n_r, n_a, n_o = velocity.shape
     rounds = SWEEPS + 1
+    chunks = n_r // UNROLL
     f32 = jnp.float32
     dma = pltpu.SemaphoreType.DMA
     in_any = pl.BlockSpec(memory_space=pl.ANY)
@@ -451,15 +478,15 @@
             pltpu.VMEM((n_r, n_a, n_o), f32),
             pltpu.VMEM((rounds, 2, (COMPS + 1) * n_r, 1, n_o), f32),
             pltpu.VMEM((rounds, 2, (COMPS + 1) * n_r, 1, n_o), f32),
-            pltpu.VMEM((rounds, 2, n_a, LANES), f32),
-            pltpu.VMEM((rounds, 2, n_a, LANES), f32),
+            pltpu.VMEM((rounds, chunks, 2, n_a, LANES), f32),
+            pltpu.VMEM((rounds, chunks, 2, n_a, LANES), f32),
             pltpu.VMEM((n_o // LANES, COMPS * (n_r // 2) * n_a, LANES), f32),
             pltpu.VMEM((n_lat, 1, LANES), f32),
             pltpu.VMEM((n_lon, 1, LANES), f32),
             pltpu.VMEM((2, 1, LANES), f32),
             dma((4,)),
-            dma((rounds, 8)),
-            dma((rounds, 8)),
+            dma((rounds, chunks, 8)),
+            dma((rounds, chunks, 8)),
             dma((n_lat,)),
             dma((n_lat,)),
             dma((n_lon * n_rad,)),

time: 25.4 us -> 23.7 us (0.933)
  Pallas kernels: 24.7 us -> 22.9 us
    pallas_call x1, Pallas kernels: 23.9 us -> 22.1 us  [on_device(): pl.pallas_call(functools.partial(kernel, sizes), out_shape=(pltpu.VMEM((C...]
where the time goes in v3:
time: 23.7 us; the launch traced here: 23.5 us
  Pallas kernels  22.9 us (97%)
  between operations  0.64 us (3%)
    pallas_call x1, Pallas kernels, on_device(): pl.pallas_call(functools.partial(kernel, sizes), out_shape=(pltpu.VMEM((C...  22.1 us
    pallas_call x1, Pallas kernels, on_device(): pl.pallas_call(write_out, out_shape=(jax.ShapeDtypeStruct(velocity.shape,...  0.8 us

profile of v3, /device:TPU:0, one launch (start us, length us, event | category | flops | bytes accessed | tf_op | source)
XLA Modules:
  0.0 23.5 jit_solution(9312185641405585895)
XLA Ops:
  0.6 22.1 %shard_map.67 = (f32[3,18,8,256]{3,2,1,0:T(8,128)S(1)}, f32[3,64,128]{2,1,0:T(8,128)S(1)}, f32[3,8,256]{2,1,0:T(8,128)S(1)}) custom-call(f32[3,16,8,256]{3,2,1,0:T(8,128)} %vel.1, f32[3,16,8,256]{3,2,1,0:T(8,128)} %forc.1, f32[16,8,256]{2,1,0:T(8,128)} %visc.1, s32[1,32]{1,0:T(1,128)} %ids_in.1), custom_call_target="tpu_custom_call" | custom-call | tf_op jit(solution)/shard_map/pallas_call | solution.py:460
  22.7 0.8 %shard_map.68 = (f32[3,16,8,256]{3,2,1,0:T(8,128)}, f32[3,64,128]{2,1,0:T(8,128)}, f32[3,8,256]{2,1,0:T(8,128)}) custom-call(f32[3,18,8,256]{3,2,1,0:T(8,128)S(1)} %get-tuple-element.9.last, f32[3,64,128]{2,1,0:T(8,128)S(1)} %get-tuple-element.10.coarse, f32[3,8,256]{2,1,0:T(8,128)S(1)} %get-tuple-element.11.plate), custom_call_target="tpu_custom_call" | custom-call | tf_op jit(solution)/shard_map/pallas_call | solution.py:504

commit v4 on v3

--- a/solution.py
+++ b/solution.py
@@ -334,7 +334,9 @@
                     tile, total = flux(t, b, j, c, cols_in)
                     fresh = (1.0 - RELAX) * tile + gain[r] * total
                     v[t + 1][c, r + 1] = fresh
-                    cols = pack(t + 1, b, j, c, fresh, cols)
+            for j in range(UNROLL):
+                for c in range(COMPS):
+                    cols = pack(t + 1, b, j, c, v[t + 1][c, b * UNROLL + j + 1], cols)
             put_cols(t + 1, b, cols)
             if t == SWEEPS - 1 and b == blocks_r - 1:
                 pl.when(is_top)(torques)

time: 23.7 us -> 23.6 us (level)
  no operation moved by 1% of the time
where the time goes in v4:
time: 23.6 us; the launch traced here: 23.5 us
  Pallas kernels  22.8 us (97%)
  between operations  0.64 us (3%)
    pallas_call x1, Pallas kernels, on_device(): pl.pallas_call(functools.partial(kernel, sizes), out_shape=(pltpu.VMEM((C...  22 us
    pallas_call x1, Pallas kernels, on_device(): pl.pallas_call(write_out, out_shape=(jax.ShapeDtypeStruct(velocity.shape,...  0.8 us

profile of v4, /device:TPU:0, one launch (start us, length us, event | category | flops | bytes accessed | tf_op | source)
XLA Modules:
  0.0 23.5 jit_solution(13255771770570919089)
XLA Ops:
  0.6 22.0 %shard_map.67 = (f32[3,18,8,256]{3,2,1,0:T(8,128)S(1)}, f32[3,64,128]{2,1,0:T(8,128)S(1)}, f32[3,8,256]{2,1,0:T(8,128)S(1)}) custom-call(f32[3,16,8,256]{3,2,1,0:T(8,128)} %vel.1, f32[3,16,8,256]{3,2,1,0:T(8,128)} %forc.1, f32[16,8,256]{2,1,0:T(8,128)} %visc.1, s32[1,32]{1,0:T(1,128)} %ids_in.1), custom_call_target="tpu_custom_call" | custom-call | tf_op jit(solution)/shard_map/pallas_call | solution.py:462
  22.7 0.8 %shard_map.68 = (f32[3,16,8,256]{3,2,1,0:T(8,128)}, f32[3,64,128]{2,1,0:T(8,128)}, f32[3,8,256]{2,1,0:T(8,128)}) custom-call(f32[3,18,8,256]{3,2,1,0:T(8,128)S(1)} %get-tuple-element.9.last, f32[3,64,128]{2,1,0:T(8,128)S(1)} %get-tuple-element.10.coarse, f32[3,8,256]{2,1,0:T(8,128)S(1)} %get-tuple-element.11.plate), custom_call_target="tpu_custom_call" | custom-call | tf_op jit(solution)/shard_map/pallas_call | solution.py:506
